TPU v7x, 32 devices: a whole 2x2x4 slice. The times are simulated.
32 devices in a mesh: row: 8 (over y, x, core), col: 4 (over z).
Axes of the slice: x: 2, y: 2, z: 4, core: 2. Of those that a mesh axis runs over, the one named last changes fastest.
Arguments:
- trailing: float32 [6144, 4096], P('row', 'col'), may hold values from -6 to 6
- column_block: bfloat16 [6144, 1024], P('row', 'col'), may hold values from -6 to 6
- row_block: bfloat16 [1024, 4096], P('row', 'col'), may hold values from -0.1875 to 0.1875
- lower_inv: bfloat16 [1024, 1024], replicated, may hold values from -1 to 1, as said below
- upper_inv: bfloat16 [1024, 1024], replicated, may hold values from -2 to 2, as said below
Outputs:
- lower_panel: bfloat16 [6144, 1024], P('row', 'col')
- upper_panel: bfloat16 [1024, 4096], P('row', 'col')
- updated: float32 [6144, 4096], P('row', 'col')
Inputs may be any that keep to these rules, and one draw needn't show every extreme that they name: `lower_inv`: lower triangular with ones on the diagonal. `upper_inv`: upper triangular with diagonal entries between 0.5 and 2.
All inputs are finite; a program needn't handle non-finite values.
Results may differ from a plain program's by a relative error of at most 0.0044.
Values may be sent and summed in bfloat16 or wider, within the bound.
A program may use at most 64 MiB of HBM per device.

v0:
```python
import jax
import jax.numpy as jnp
from jax import lax
from jax.sharding import PartitionSpec as P


def on_device(trailing, column_block, row_block, lower_inv, upper_inv):
    col_share = column_block.shape[1]
    row_share = row_block.shape[0]
    col_start = lax.axis_index("col") * col_share
    row_start = lax.axis_index("row") * row_share
    factor = upper_inv
    lower_full = jnp.dot(
        lax.all_gather(column_block, "col", axis=1, tiled=True),
        factor,
        preferred_element_type=jnp.float32,
    ).astype(jnp.bfloat16)
    factor = lower_inv
    upper_full = jnp.dot(
        factor,
        lax.all_gather(row_block, "row", axis=0, tiled=True),
        preferred_element_type=jnp.float32,
    ).astype(jnp.bfloat16)
    product = jnp.dot(lower_full, upper_full, preferred_element_type=jnp.float32)
    lower_tile = lax.dynamic_slice_in_dim(lower_full, col_start, col_share, 1)
    upper_tile = lax.dynamic_slice_in_dim(upper_full, row_start, row_share, 0)
    updated = trailing - product
    return (lower_tile, upper_tile, updated)


def solution(mesh):
    in_specs = (P("row", "col"), P("row", "col"), P("row", "col"), P(), P())
    out_specs = (P("row", "col"), P("row", "col"), P("row", "col"))
    return jax.shard_map(
        on_device, mesh=mesh, in_specs=in_specs, out_specs=out_specs, check_vma=False
    )
```

profile of v0, /device:TPU:0, one launch (start us, length us, event | category | flops | bytes accessed | tf_op | source)
XLA Modules:
  0.0 93.0 jit_solution(8704201044639735974)
XLA Ops:
  7.2 0.0 copy-start
  7.2 0.0 all-gather.3.cloned.1.call-start
  7.2 0.7 all-gather.3.cloned.1.call-update
  7.9 0.0 all-gather.5.cloned.1.call-start
  8.0 0.7 all-gather.5.cloned.1.call-update
  8.7 41.3 %all-gather.3.cloned.1.call-done = bf16[768,1024]{1,0:T(8,128)(2,1)} async-done(((bf16[768,256]{1,0:T(8,128)(2,1)}), bf16[768,1024]{1,0:T(8,128)(2,1)}) %all-gather.3.cloned.1.call-update) | async-done | bytes 1572880 | tf_op jit(solution)/shard_map/all_gather | solution.py:14
  50.0 3.9 %convolution_convert_fusion.1 = bf16[768,1024]{1,0:T(8,128)(2,1)S(1)} fusion(bf16[768,1024]{1,0:T(8,128)(2,1)} %all-gather.3.cloned.1.call-done, bf16[1024,1024]{1,0:T(8,128)(2,1)} %param.9), kind=kOutput, calls=%fused_computation.2 | convolution fusion | flops 1611399168 | bytes 5242880 | tf_op jit(solution)/shard_map/dot_general | solution.py:13
  53.9 0.0 copy-start.1
  53.9 1.1 %copy-done.1 = bf16[768,1024]{1,0:T(8,128)(2,1)} copy-done((bf16[768,1024]{1,0:T(8,128)(2,1)}, bf16[768,1024]{1,0:T(8,128)(2,1)S(1)}, u32[]{:S(2)}) %copy-start.1) | copy-done | bytes 1572888
  55.0 0.8 constant_dynamic-slice_fusion.1
  55.8 22.1 %all-gather.5.cloned.1.call-done = bf16[1024,1024]{1,0:T(8,128)(2,1)} async-done(((bf16[128,1024]{1,0:T(8,128)(2,1)}), bf16[1024,1024]{1,0:T(8,128)(2,1)}) %all-gather.5.cloned.1.call-update) | async-done | bytes 2097168 | tf_op jit(solution)/shard_map/all_gather | solution.py:21
  77.9 0.0 copy-done
  77.9 0.0 copy-start.2
  77.9 0.0 copy-start.3
  77.9 4.1 %convolution_convert_fusion = bf16[1024,1024]{1,0:T(8,128)(2,1)S(1)} fusion(bf16[1024,1024]{1,0:T(8,128)(2,1)S(1)} %copy-done, bf16[1024,1024]{1,0:T(8,128)(2,1)} %all-gather.5.cloned.1.call-done), kind=kOutput, calls=%fused_computation | convolution fusion | flops 2148532224 | bytes 6291456 | tf_op jit(solution)/shard_map/dot_general | solution.py:19
  82.0 0.7 constant_dynamic-slice_fusion
  82.7 0.0 copy-done.2
  82.7 0.0 copy-done.3
  82.7 3.5 %convolution_subtract_fusion = f32[768,1024]{1,0:T(8,128)} fusion(f32[768,1024]{1,0:T(8,128)S(1)} %copy-done.3, bf16[768,1024]{1,0:T(8,128)(2,1)S(1)} %copy-done.2, bf16[1024,1024]{1,0:T(8,128)(2,1)S(1)} %convolution_convert_fusion), kind=kOutput, calls=%fused_computation.1 | convolution fusion | flops 1611399168 | bytes 9961472 | tf_op jit(solution)/shard_map/dot_general | solution.py:24
Async XLA Ops:
  7.2 70.8 %copy-start = (bf16[1024,1024]{1,0:T(8,128)(2,1)S(1)}, bf16[1024,1024]{1,0:T(8,128)(2,1)}, u32[]{:S(2)}) copy-start(bf16[1024,1024]{1,0:T(8,128)(2,1)} %param.8) | copy-start | bytes 6291460
  7.2 42.8 %all-gather.3.cloned.1.call-start = ((), (), s32[]{:S(2)}) async-start(), calls=%async_computation | async-start | bytes 1966080 | tf_op jit(solution)/shard_map/all_gather | solution.py:14
  7.9 70.0 %all-gather.5.cloned.1.call-start = ((), (), s32[]{:S(2)}) async-start(), calls=%async_computation.1 | async-start | bytes 2359296 | tf_op jit(solution)/shard_map/all_gather | solution.py:21
  53.9 1.1 %copy-start.1 = (bf16[768,1024]{1,0:T(8,128)(2,1)}, bf16[768,1024]{1,0:T(8,128)(2,1)S(1)}, u32[]{:S(2)}) copy-start(bf16[768,1024]{1,0:T(8,128)(2,1)S(1)} %convolution_convert_fusion.1) | copy-start | bytes 4718596
  77.9 4.8 %copy-start.2 = (bf16[768,1024]{1,0:T(8,128)(2,1)S(1)}, bf16[768,1024]{1,0:T(8,128)(2,1)}, u32[]{:S(2)}) copy-start(bf16[768,1024]{1,0:T(8,128)(2,1)} %copy-done.1) | copy-start | bytes 4718596
  77.9 4.8 %copy-start.3 = (f32[768,1024]{1,0:T(8,128)S(1)}, f32[768,1024]{1,0:T(8,128)}, u32[]{:S(2)}) copy-start(f32[768,1024]{1,0:T(8,128)} %param.5) | copy-start | bytes 9437188
Sparse Core Ops, SparseCore 0:
  9.5 40.3 all-gather.2
  51.9 25.9 all-gather.4
where the time goes:
time: 93.2 us; the launch traced here: 93 us
  waiting for transfers between devices  64.8 us (70%)
  between operations  14.1 us (15%)
  matrix products  11.4 us (12%)
  local copies, waits for them, and re-layouts  2.68 us (3%)
    all_gather x1, waiting for transfers between devices, on_device(): lax.all_gather(column_block, 'col', axis=1, tiled=True)  41.3 us
    all_gather x1, waiting for transfers between devices, on_device(): lax.all_gather(row_block, 'row', axis=0, tiled=True)  22.1 us
    dot_general x1, matrix products, on_device(): jnp.dot(factor, lax.all_gather(row_block, 'row', axis=0, tiled=True), pre...  4.06 us
    dot_general x1, matrix products, on_device(): jnp.dot(lax.all_gather(column_block, 'col', axis=1, tiled=True), factor,...  3.86 us
    dot_general x1, matrix products, on_device(): jnp.dot(lower_full, upper_full, preferred_element_type=jnp.float32)  3.47 us
  transfers between devices with their start and end apart: 2, of which 2 were waited for; matrix products, arithmetic and copies ran while one was open for 5% of the time, Pallas kernels for 0%

commit v1 on v0

--- a/solution.py
+++ b/solution.py
@@ -2,6 +2,13 @@
 import jax.numpy as jnp
 from jax import lax
 from jax.sharding import PartitionSpec as P
+
+
+def all_by_exchange(value, mesh_axis, dim):
+    devices = lax.axis_size(mesh_axis)
+    shards = jnp.stack([value for _ in range(devices)])
+    shards = lax.all_to_all(shards, mesh_axis, split_axis=0, concat_axis=0)
+    return jnp.concatenate(shards, axis=dim)
 
 
 def on_device(trailing, column_block, row_block, lower_inv, upper_inv):
@@ -17,9 +24,7 @@
     ).astype(jnp.bfloat16)
     factor = lower_inv
     upper_full = jnp.dot(
-        factor,
-        lax.all_gather(row_block, "row", axis=0, tiled=True),
-        preferred_element_type=jnp.float32,
+        factor, all_by_exchange(row_block, "row", 0), preferred_element_type=jnp.float32
     ).astype(jnp.bfloat16)
     product = jnp.dot(lower_full, upper_full, preferred_element_type=jnp.float32)
     lower_tile = lax.dynamic_slice_in_dim(lower_full, col_start, col_share, 1)

time: 93.2 us -> 72.8 us (0.78)
  waiting for transfers between devices: 64.8 us -> 36.3 us
  starting transfers between devices: 0.08 us -> 5.24 us
  local copies, waits for them, and re-layouts: 2.68 us -> 5.54 us
    all_gather x1, waiting for transfers between devices: 41.3 us -> 9.63 us  [on_device(): lax.all_gather(column_block, 'col', axis=1, tiled=True)]
    all_to_all x0 -> x1, waiting for transfers between devices: none -> 26 us  [all_by_exchange(): shards = lax.all_to_all(shards, mesh_axis, split_axis=0, concat_axis=0)]
    all_gather x1 -> x0, waiting for transfers between devices: 22.1 us -> none  [on_device(): lax.all_gather(row_block, 'row', axis=0, tiled=True)]
    all_to_all x0 -> x1, starting transfers between devices: none -> 5.2 us  [all_by_exchange(): shards = lax.all_to_all(shards, mesh_axis, split_axis=0, concat_axis=0)]
    another operation x0 -> x1, local copies, waits for them, and re-layouts: none -> 2.68 us  [all_by_exchange(): shards = jnp.stack([value for _ in range(devices)])]
  transfers between devices with their start and end apart: 2 -> 2, of which waited for: 2 -> 2; matrix products, arithmetic and copies ran while one was open for 5% -> 6% of each run, Pallas kernels for 0% -> 0%
where the time goes in v1:
time: 72.8 us; the launch traced here: 72.5 us
  waiting for transfers between devices  36.3 us (50%)
  between operations  14.1 us (19%)
  matrix products  11.4 us (16%)
  local copies, waits for them, and re-layouts  5.54 us (8%)
  starting transfers between devices  5.24 us (7%)
    all_to_all x1, waiting for transfers between devices, all_by_exchange(): shards = lax.all_to_all(shards, mesh_axis, split_axis=0, concat_axis=0)  26 us
    all_gather x1, waiting for transfers between devices, on_device(): lax.all_gather(column_block, 'col', axis=1, tiled=True)  9.63 us
    all_to_all x1, starting transfers between devices, all_by_exchange(): shards = lax.all_to_all(shards, mesh_axis, split_axis=0, concat_axis=0)  5.2 us
    dot_general x1, matrix products, on_device(): jnp.dot(lax.all_gather(column_block, 'col', axis=1, tiled=True), factor,...  4 us
    dot_general x1, matrix products, on_device(): jnp.dot(factor, all_by_exchange(row_block, 'row', 0), preferred_element_t...  3.93 us
    dot_general x1, matrix products, on_device(): jnp.dot(lower_full, upper_full, preferred_element_type=jnp.float32)  3.47 us
    another operation x1, local copies, waits for them, and re-layouts, all_by_exchange(): shards = jnp.stack([value for _ in range(devices)])  2.68 us
  transfers between devices with their start and end apart: 2, of which 2 were waited for; matrix products, arithmetic and copies ran while one was open for 6% of the time, Pallas kernels for 0%

profile of v1, /device:TPU:0, one launch (start us, length us, event | category | flops | bytes accessed | tf_op | source)
XLA Modules:
  0.0 72.5 jit_solution(11361054811743715471)
XLA Ops:
  7.2 0.0 copy-start
  7.2 2.7 %stack.2 = bf16[8,128,1024]{2,1,0:T(8,128)(2,1)} broadcast(bf16[128,1024]{1,0:T(8,128)(2,1)} %param.7), dimensions={1,2} | broadcast | bytes 2359296 | tf_op jit(solution)/shard_map/stack | solution.py:9
  9.9 5.2 %all-to-all-start = ((bf16[8,128,1024]{2,1,0:T(8,128)(2,1)}), bf16[8,128,1024]{2,1,0:T(8,128)(2,1)}, u32[]{:S(2)}, u32[]{:S(2)}) async-start(bf16[8,128,1024]{2,1,0:T(8,128)(2,1)} %stack.2), calls=%async_computation | async-start | bytes 4194304 | tf_op jit(solution)/shard_map/all_to_all | solution.py:10
  15.1 0.0 all-gather.2.cloned.1.call-start
  15.1 0.7 all-gather.2.cloned.1.call-update
  15.8 26.0 %all-to-all-done = bf16[8,128,1024]{2,1,0:T(8,128)(2,1)} async-done(((bf16[8,128,1024]{2,1,0:T(8,128)(2,1)}), bf16[8,128,1024]{2,1,0:T(8,128)(2,1)}, u32[]{:S(2)}, u32[]{:S(2)}) %all-to-all-start) | async-done | bytes 2097184 | tf_op jit(solution)/shard_map/all_to_all | solution.py:10
  41.8 0.0 copy-done
  41.8 3.9 %convolution_convert_fusion = bf16[1024,1024]{1,0:T(8,128)(2,1)S(1)} fusion(bf16[1024,1024]{1,0:T(8,128)(2,1)S(1)} %copy-done, bf16[1024,1024]{1,0:T(8,128)(2,1)} %bitcast), kind=kOutput, calls=%fused_computation | convolution fusion | flops 2148532224 | bytes 6291456 | tf_op jit(solution)/shard_map/dot_general | solution.py:26
  45.7 0.0 copy-start.1
  45.7 1.3 %copy-done.1 = bf16[1024,1024]{1,0:T(8,128)(2,1)} copy-done((bf16[1024,1024]{1,0:T(8,128)(2,1)}, bf16[1024,1024]{1,0:T(8,128)(2,1)S(1)}, u32[]{:S(2)}) %copy-start.1) | copy-done | bytes 2097176
  47.0 0.7 constant_dynamic-slice_fusion
  47.8 9.6 %all-gather.2.cloned.1.call-done = bf16[768,1024]{1,0:T(8,128)(2,1)} async-done(((bf16[768,256]{1,0:T(8,128)(2,1)}), bf16[768,1024]{1,0:T(8,128)(2,1)}) %all-gather.2.cloned.1.call-update) | async-done | bytes 1572880 | tf_op jit(solution)/shard_map/all_gather | solution.py:21
  57.4 0.0 copy-start.2
  57.4 0.0 copy-start.3
  57.4 4.0 %convolution_convert_fusion.1 = bf16[768,1024]{1,0:T(8,128)(2,1)S(1)} fusion(bf16[768,1024]{1,0:T(8,128)(2,1)} %all-gather.2.cloned.1.call-done, bf16[1024,1024]{1,0:T(8,128)(2,1)} %param.9), kind=kOutput, calls=%fused_computation.2 | convolution fusion | flops 1611399168 | bytes 5242880 | tf_op jit(solution)/shard_map/dot_general | solution.py:20
  61.4 0.8 %constant_dynamic-slice_fusion.1 = bf16[768,256]{1,0:T(8,128)(2,1)} fusion(bf16[768,1024]{1,0:T(8,128)(2,1)S(1)} %convolution_convert_fusion.1, s32[]{:T(128)S(6)} %select_n.6), kind=kLoop, calls=%fused_computation.4 | loop fusion | bytes 786436 | tf_op jit(solution)/shard_map/dynamic_slice | solution.py:30
  62.2 0.0 copy-done.2
  62.2 0.0 copy-done.3
  62.2 3.5 %convolution_subtract_fusion = f32[768,1024]{1,0:T(8,128)} fusion(f32[768,1024]{1,0:T(8,128)S(1)} %copy-done.3, bf16[768,1024]{1,0:T(8,128)(2,1)S(1)} %convolution_convert_fusion.1, bf16[1024,1024]{1,0:T(8,128)(2,1)S(1)} %copy-done.2), kind=kOutput, calls=%fused_computation.1 | convolution fusion | flops 1611399168 | bytes 9961472 | tf_op jit(solution)/shard_map/dot_general | solution.py:29
Async XLA Ops:
  7.2 34.6 %copy-start = (bf16[1024,1024]{1,0:T(8,128)(2,1)S(1)}, bf16[1024,1024]{1,0:T(8,128)(2,1)}, u32[]{:S(2)}) copy-start(bf16[1024,1024]{1,0:T(8,128)(2,1)} %param.8) | copy-start | bytes 6291460
  9.9 31.9 %all-to-all-start = ((bf16[8,128,1024]{2,1,0:T(8,128)(2,1)}), bf16[8,128,1024]{2,1,0:T(8,128)(2,1)}, u32[]{:S(2)}, u32[]{:S(2)}) async-start(bf16[8,128,1024]{2,1,0:T(8,128)(2,1)} %stack.2), calls=%async_computation | async-start | bytes 4194304 | tf_op jit(solution)/shard_map/all_to_all | solution.py:10
  15.1 42.3 %all-gather.2.cloned.1.call-start = ((), (), s32[]{:S(2)}) async-start(), calls=%async_computation.1 | async-start | bytes 1966080 | tf_op jit(solution)/shard_map/all_gather | solution.py:21
  45.7 1.3 %copy-start.1 = (bf16[1024,1024]{1,0:T(8,128)(2,1)}, bf16[1024,1024]{1,0:T(8,128)(2,1)S(1)}, u32[]{:S(2)}) copy-start(bf16[1024,1024]{1,0:T(8,128)(2,1)S(1)} %convolution_convert_fusion) | copy-start | bytes 6291460
  57.4 4.8 %copy-start.2 = (bf16[1024,1024]{1,0:T(8,128)(2,1)S(1)}, bf16[1024,1024]{1,0:T(8,128)(2,1)}, u32[]{:S(2)}) copy-start(bf16[1024,1024]{1,0:T(8,128)(2,1)} %copy-done.1) | copy-start | bytes 6291460
  57.4 4.8 %copy-start.3 = (f32[768,1024]{1,0:T(8,128)S(1)}, f32[768,1024]{1,0:T(8,128)}, u32[]{:S(2)}) copy-start(f32[768,1024]{1,0:T(8,128)} %param.5) | copy-start | bytes 9437188
Sparse Core Ops, SparseCore 0:
  17.4 39.9 all-gather.1
